TPU v7x, 256 devices: a whole 4x4x8 slice. The times are simulated.
256 devices in a mesh: st: 16 (over y, x), tp: 16 (over z, core).
Axes of the slice: x: 4, y: 4, z: 8, core: 2. Of those that a mesh axis runs over, the one named last changes fastest.
Arguments:
- continuous: bfloat16 [512, 3, 1424], P(('st', 'tp')), may hold values from -48 to 48
- templates: bfloat16 [512, 12, 3, 400], P(('st', 'tp')), may hold values from -120 to 120
- station_list: int32 [512, 12], P(('st', 'tp')), may hold values from 0 to 511, as said below
- moveouts: int32 [512, 12], P(('st', 'tp')), may hold values from 0 to 256
Outputs:
- detection: float32 [512, 768], P(('st', 'tp'))
Inputs may be any that keep to these rules, and one draw needn't show every extreme that they name: `station_list`: A station's group is station // 32. The 12 stations of a template are distinct, and so are their indices within their groups (station % 32). The rows of one device (2 templates, aligned blocks in order) name at most 3 stations of any one group, and in every such block one group is named exactly 3 times; blocks b and b2 with b % 16 == b2 % 16 share that group.
All inputs are finite; a program needn't handle non-finite values.
Results may differ from a plain program's by a relative error of at most 0.0003.
Values may be sent and summed in bfloat16 or wider, within the bound.
No kernel may reach another device: no remote copies, remote signals or barrier semaphores. Data moves between devices by JAX's collectives and lax.ppermute only.
A program may use at most 64 MiB of HBM per device.

v0:
```python
import math
import jax
import jax.numpy as jnp
from jax import lax
from jax.sharding import PartitionSpec as P

WIN = 768
TLEN = 400
CH = 3
OUT = 1024
EPS = 1e-05


def frame_width():
    return 128


def toeplitz(vector, row_width, frame_size):
    leading = vector.shape[:-1]
    padded = jnp.concatenate(
        [vector, jnp.zeros(leading + (row_width + 1 - vector.shape[-1],), vector.dtype)], axis=-1
    )
    repeated = jnp.tile(padded, (1,) * len(leading) + (frame_size,))
    return repeated[..., : frame_size * row_width].reshape(leading + (frame_size, row_width))


def to_frames(series, frame_size, frame_count):
    target = frame_size * frame_count
    length_now = series.shape[-1]
    if length_now >= target:
        fitted = series[..., :target]
    else:
        fitted = jnp.concatenate(
            [series, jnp.zeros(series.shape[:-1] + (target - length_now,), series.dtype)], axis=-1
        )
    return fitted.reshape(series.shape[:-1] + (frame_count, frame_size))


def inverse_level(row_data):
    squares = jnp.square(row_data.astype(jnp.float32))
    running = jnp.cumsum(squares, axis=-1)
    running = jnp.concatenate([jnp.zeros(running.shape[:-1] + (1,), jnp.float32), running], axis=-1)
    energy = running[..., TLEN : TLEN + OUT] - running[..., :OUT]
    return lax.rsqrt(energy / TLEN + EPS)


def correlate(templates, row_data, inverse, shifts):
    frame_size = frame_width()
    blocks = OUT // frame_size
    step_count = (TLEN + 2 * frame_size - 2) // frame_size
    frames = to_frames(row_data, frame_size, blocks + step_count - 1)
    bands = toeplitz(templates, step_count * frame_size, frame_size)
    running = jnp.zeros(templates.shape[:-1] + (blocks, frame_size), jnp.float32)
    for step_index in range(step_count):
        running = running + jnp.einsum(
            "ncbp,ncip->ncbi",
            frames[:, :, step_index : step_index + blocks],
            bands[..., step_index * frame_size : (step_index + 1) * frame_size],
            preferred_element_type=jnp.float32,
        )
    raw_sums = running.reshape(templates.shape[:-1] + (OUT,))
    template_values = templates.astype(jnp.float32)
    template_inverse = lax.rsqrt(jnp.mean(template_values * template_values, axis=-1) + EPS)
    scaled = raw_sums * inverse * (template_inverse / TLEN)[..., None]
    summed = jnp.sum(scaled, axis=1)
    return jax.vmap(lambda series, start_at: lax.dynamic_slice_in_dim(series, start_at, WIN))(
        summed, shifts
    )


def in_blocks(worker, arrays, item_count):
    block_size = math.gcd(item_count, 32)
    grouped = jax.tree.map(
        lambda member: member.reshape((item_count // block_size, block_size) + member.shape[1:]),
        arrays,
    )
    result = lax.map(worker, grouped)
    return result.reshape((item_count,) + result.shape[2:])


def shards(continuous, templates, station_list, moveouts):
    group_count = lax.axis_size("st")
    template_count = templates.shape[0]
    list_size = templates.shape[1]
    group_size = continuous.shape[0] * lax.axis_size("tp")
    entries = template_count * list_size
    capacity = 2 * entries // group_count
    slots_total = group_count * capacity
    flat_list = station_list.reshape(entries)
    owners = flat_list // group_size
    within = flat_list - owners * group_size
    member = (owners[:, None] == jnp.arange(group_count, dtype=jnp.int32)[None, :]).astype(
        jnp.int32
    )
    earlier = jnp.cumsum(member, axis=0) - member
    position = jnp.sum(earlier * member, axis=1)
    slot_index = owners * capacity + position
    flat_shift = moveouts.reshape(entries)
    flat_templates = templates.reshape(entries, CH, TLEN)
    group_rows = lax.all_gather(continuous, "tp", axis=0, tiled=True)
    local_scale = inverse_level(continuous)
    group_scale = lax.all_gather(local_scale, "tp", axis=0, tiled=True)
    slot_templates = (
        jnp.zeros((slots_total, CH, TLEN), jnp.bfloat16)
        .at[slot_index]
        .set(flat_templates)
        .reshape(group_count, capacity, CH, TLEN)
    )
    slot_station = (
        jnp.zeros((slots_total,), jnp.int32)
        .at[slot_index]
        .set(within)
        .reshape(group_count, capacity)
    )
    slot_shift = (
        jnp.zeros((slots_total,), jnp.int32)
        .at[slot_index]
        .set(flat_shift)
        .reshape(group_count, capacity)
    )
    template_rows = jnp.arange(entries, dtype=jnp.int32) // list_size
    slot_row = (
        jnp.full((slots_total,), -1, jnp.int32)
        .at[slot_index]
        .set(template_rows)
        .reshape(group_count, capacity)
    )
    pieces = (
        lax.all_to_all(slot_templates, "st", split_axis=0, concat_axis=0, tiled=True),
        lax.all_to_all(slot_station, "st", split_axis=0, concat_axis=0, tiled=True),
        lax.all_to_all(slot_shift, "st", split_axis=0, concat_axis=0, tiled=True),
        lax.all_to_all(slot_row, "st", split_axis=0, concat_axis=0, tiled=True),
    )
    given_items = pieces[1].shape[1]
    item_total = group_count * given_items
    stations = pieces[1].reshape(item_total)

    def block_work(block_parts):
        picked = group_rows[block_parts[1]]
        scales = group_scale[block_parts[1]]
        return correlate(block_parts[0], picked, scales, block_parts[2])

    aligned = in_blocks(
        block_work,
        (pieces[0].reshape(item_total, CH, TLEN), stations, pieces[2].reshape(item_total)),
        item_total,
    )
    aligned = aligned.reshape(group_count, given_items, WIN)
    outcome = lax.all_to_all(aligned, "st", split_axis=0, concat_axis=0, tiled=True)
    returned = outcome.reshape(slots_total, WIN)
    detection = jnp.sum(returned[slot_index].reshape(template_count, list_size, WIN), axis=1)
    return detection


def solution(mesh):
    placed = (
        P(("st", "tp"), None, None),
        P(("st", "tp"), None, None, None),
        P(("st", "tp"), None),
        P(("st", "tp"), None),
    )
    return jax.shard_map(
        shards, mesh=mesh, in_specs=placed, out_specs=P(("st", "tp"), None), check_vma=False
    )
```

profile of v0, /device:TPU:1, one launch (start us, length us, event | category | flops | bytes accessed | tf_op | source)
XLA Modules:
  0.0 315.8 jit_solution(9241197503857095357)
XLA Ops:
  3.2 7.6 %all-to-all-start = ((s32[16,1,3]{2,1,0:T(1,128)}), s32[16,1,3]{2,1,0:T(1,128)S(1)}, u32[]{:S(2)}, u32[]{:S(2)}) async-start(s32[16,1,3]{2,1,0:T(1,128)} %bitcast.7), calls=%async_computation | async-start | bytes 16384 | tf_op jit(solution)/shard_map/all_to_all | solution.py:130
  13.8 1.7 reduce-window.6
  16.6 22.2 %all_gather.7 = f32[32,3,1024]{2,1,0:T(4,128)S(1)} all-gather(f32[2,3,1024]{2,1,0:T(4,128)S(1)} %copy.76), channel_id=1, replica_groups=mesh['st'=16,'tp'=16] {'tp'}, dimensions={0}, use_global_device_ids=true | all-gather | bytes 417792 | tf_op jit(solution)/shard_map/all_gather | solution.py:102
  39.6 6.9 %all-to-all-start.2 = ((s32[16,1,3]{2,1,0:T(1,128)}), s32[16,1,3]{2,1,0:T(1,128)S(1)}, u32[]{:S(2)}, u32[]{:S(2)}) async-start(s32[16,1,3]{2,1,0:T(1,128)} %bitcast.11), calls=%async_computation.2 | async-start | bytes 16384 | tf_op jit(solution)/shard_map/all_to_all | solution.py:131
  46.6 1.5 scatter_fusion
  48.9 3.9 %all-to-all-done.2 = s32[16,1,3]{2,1,0:T(1,128)S(1)} async-done(((s32[16,1,3]{2,1,0:T(1,128)}), s32[16,1,3]{2,1,0:T(1,128)S(1)}, u32[]{:S(2)}, u32[]{:S(2)}) %all-to-all-start.2) | async-done | bytes 224 | tf_op jit(solution)/shard_map/all_to_all | solution.py:131
  52.8 3.5 %all-to-all-start.1 = ((bf16[16,3,3,400]{3,1,2,0:T(4,128)(2,1)}), bf16[16,3,3,400]{3,1,2,0:T(4,128)(2,1)S(1)}, u32[]{:S(2)}, u32[]{:S(2)}) async-start(bf16[16,3,3,400]{3,1,2,0:T(4,128)(2,1)} %copy.70), calls=%async_computation.1 | async-start | bytes 393216 | tf_op jit(solution)/shard_map/all_to_all | solution.py:129
  56.3 16.9 %all_gather.6 = bf16[32,3,1424]{2,1,0:T(4,128)(2,1)S(1)} all-gather(bf16[2,3,1424]{2,1,0:T(4,128)(2,1)S(1)} %copy.67), channel_id=1, replica_groups=mesh['st'=16,'tp'=16] {'tp'}, dimensions={0}, use_global_device_ids=true | all-gather | bytes 290496 | tf_op jit(solution)/shard_map/all_gather | solution.py:100
  75.9 222.4 %while.13 = (s32[]{:T(128)}, f32[3,16,768]{2,1,0:T(8,128)}, s32[3,16]{1,0:T(4,128)S(1)}, bf16[32,3,1424]{2,1,0:T(4,128)(2,1)S(1)}, bf16[3,16,3,400]{3,1,0,2:T(8,...) while((s32[]{:T(128)}, f32[3,16,768]{2,1,0:T(8,128)}, ...), condition=%wide.region_10.11_spmd, body=%wide.region_7.10_spmd.sunk | while | flops 63301088 | bytes 91004616 | solution.py:77
  77.8 4.3 %tile.11 = bf16[16,3,128,641]{3,2,0,1:T(8,128)(2,1)} broadcast(bf16[16,3,641]{2,0,1:T(8,128)(2,1)S(1)} %concatenate.21), dimensions={0,1,3} | broadcast | bytes 7938144 | tf_op jit(solution)/shard_map/while/body/eval_jaxpr/tile | solution.py:23
  82.1 14.9 %tile.12 = bf16[16,3,82048]{2,0,1:T(8,128)(2,1)} reshape(bf16[16,3,128,641]{3,2,0,1:T(8,128)(2,1)} %tile.11) | data formatting | bytes 15753216 | tf_op jit(solution)/shard_map/while/body/eval_jaxpr/tile | solution.py:23
  97.0 3.2 %slice-done = bf16[16,3,81920]{2,0,1:T(8,128)(2,1)S(1)} async-done(((bf16[16,3,82048]{2,0,1:T(8,128)(2,1)}), bf16[16,3,81920]{2,0,1:T(8,128)(2,1)S(1)}, s32[]{:S(2)}) %slice-start) | async-done | bytes 7864344 | tf_op jit(solution)/shard_map/while/body/eval_jaxpr/slice | solution.py:24
  100.2 4.6 %copy.136 = bf16[6,8,128,640]{3,2,1,0:T(8,128)(2,1)} copy(bf16[6,8,128,640]{3,1,2,0:T(8,128)(2,1)S(1)} %bitcast.72) | data formatting | bytes 15728640 | tf_op jit(solution)/shard_map/while
  104.8 3.7 %fusion.78 = (bf16[16,3,128,128]{3,2,0,1:T(8,128)(2,1)S(1)}, bf16[16,3,128,128]{3,2,0,1:T(8,128)(2,1)S(1)}, bf16[16,3,128,128]{3,2,0,1:T(8,128)(2,1)S(1)}, bf16[...) fusion(bf16[16,3,128,640]{3,2,0,1:T(8,128)(2,1)} %bitcast.73), kind=kLoop, calls=%fused_computation.70.clone.1 | loop fusion | bytes 15728640 | tf_op jit(solution)/shard_map/while/body/eval_jaxpr/slice | solution.py:58
  114.1 35.3 %while.14 = (s32[]{:T(128)}, f32[16,1024]{1,0:T(8,128)S(1)}, s32[16,2]{0,1:T(2,128)S(1)}, f32[16,768]{1,0:T(8,128)S(1)}, s32[]{:T(128)}, /*index=5*/s32[]{:T(128)}) while((s32[]{:T(128)}, f32[16,1024]{1,0:T(8,128)S(1)}, s32[16,2]{0,1:T(2,128)S(1)}, f32[16,768]{1,0:T(8,128)S(1)}, s32[]{:T(128)}, /*index=5*/s32[]{:T(128)}) %tuple.55), condition=%wide.while_cond, body=%wide.while_body.sunk | while | flops 2 | bytes 12401 | solution.py:66
  114.8 1.5 dynamic-slice.7
  117.0 1.5 dynamic-slice.7
  119.2 1.5 dynamic-slice.7
  121.4 1.5 dynamic-slice.7
  123.6 1.5 dynamic-slice.7
  125.9 1.5 dynamic-slice.7
  128.1 1.5 dynamic-slice.7
  130.3 1.5 dynamic-slice.7
  132.5 1.5 dynamic-slice.7
  134.7 1.5 dynamic-slice.7
  136.9 1.5 dynamic-slice.7
  139.1 1.5 dynamic-slice.7
  141.3 1.5 dynamic-slice.7
  143.5 1.5 dynamic-slice.7
  145.7 1.5 dynamic-slice.7
  147.9 1.5 dynamic-slice.7
  152.0 4.3 %tile.11 = bf16[16,3,128,641]{3,2,0,1:T(8,128)(2,1)} broadcast(bf16[16,3,641]{2,0,1:T(8,128)(2,1)S(1)} %concatenate.21), dimensions={0,1,3} | broadcast | bytes 7938144 | tf_op jit(solution)/shard_map/while/body/eval_jaxpr/tile | solution.py:23
  156.2 14.9 %tile.12 = bf16[16,3,82048]{2,0,1:T(8,128)(2,1)} reshape(bf16[16,3,128,641]{3,2,0,1:T(8,128)(2,1)} %tile.11) | data formatting | bytes 15753216 | tf_op jit(solution)/shard_map/while/body/eval_jaxpr/tile | solution.py:23
  171.1 3.2 %slice-done = bf16[16,3,81920]{2,0,1:T(8,128)(2,1)S(1)} async-done(((bf16[16,3,82048]{2,0,1:T(8,128)(2,1)}), bf16[16,3,81920]{2,0,1:T(8,128)(2,1)S(1)}, s32[]{:S(2)}) %slice-start) | async-done | bytes 7864344 | tf_op jit(solution)/shard_map/while/body/eval_jaxpr/slice | solution.py:24
  174.4 4.6 %copy.136 = bf16[6,8,128,640]{3,2,1,0:T(8,128)(2,1)} copy(bf16[6,8,128,640]{3,1,2,0:T(8,128)(2,1)S(1)} %bitcast.72) | data formatting | bytes 15728640 | tf_op jit(solution)/shard_map/while
  178.9 3.7 %fusion.78 = (bf16[16,3,128,128]{3,2,0,1:T(8,128)(2,1)S(1)}, bf16[16,3,128,128]{3,2,0,1:T(8,128)(2,1)S(1)}, bf16[16,3,128,128]{3,2,0,1:T(8,128)(2,1)S(1)}, bf16[...) fusion(bf16[16,3,128,640]{3,2,0,1:T(8,128)(2,1)} %bitcast.73), kind=kLoop, calls=%fused_computation.70.clone.1 | loop fusion | bytes 15728640 | tf_op jit(solution)/shard_map/while/body/eval_jaxpr/slice | solution.py:58
  188.3 35.3 %while.14 = (s32[]{:T(128)}, f32[16,1024]{1,0:T(8,128)S(1)}, s32[16,2]{0,1:T(2,128)S(1)}, f32[16,768]{1,0:T(8,128)S(1)}, s32[]{:T(128)}, /*index=5*/s32[]{:T(128)}) while((s32[]{:T(128)}, f32[16,1024]{1,0:T(8,128)S(1)}, s32[16,2]{0,1:T(2,128)S(1)}, f32[16,768]{1,0:T(8,128)S(1)}, s32[]{:T(128)}, /*index=5*/s32[]{:T(128)}) %tuple.55), condition=%wide.while_cond, body=%wide.while_body.sunk | while | flops 2 | bytes 12401 | solution.py:66
  189.0 1.5 dynamic-slice.7
  191.2 1.5 dynamic-slice.7
  193.4 1.5 dynamic-slice.7
  195.6 1.5 dynamic-slice.7
  197.8 1.5 dynamic-slice.7
  200.0 1.5 dynamic-slice.7
  202.2 1.5 dynamic-slice.7
  204.4 1.5 dynamic-slice.7
  206.6 1.5 dynamic-slice.7
  208.8 1.5 dynamic-slice.7
  211.0 1.5 dynamic-slice.7
  213.2 1.5 dynamic-slice.7
  215.4 1.5 dynamic-slice.7
  217.7 1.5 dynamic-slice.7
  219.9 1.5 dynamic-slice.7
  226.1 4.3 %tile.11 = bf16[16,3,128,641]{3,2,0,1:T(8,128)(2,1)} broadcast(bf16[16,3,641]{2,0,1:T(8,128)(2,1)S(1)} %concatenate.21), dimensions={0,1,3} | broadcast | bytes 7938144 | tf_op jit(solution)/shard_map/while/body/eval_jaxpr/tile | solution.py:23
  230.4 14.9 %tile.12 = bf16[16,3,82048]{2,0,1:T(8,128)(2,1)} reshape(bf16[16,3,128,641]{3,2,0,1:T(8,128)(2,1)} %tile.11) | data formatting | bytes 15753216 | tf_op jit(solution)/shard_map/while/body/eval_jaxpr/tile | solution.py:23
  245.3 3.2 %slice-done = bf16[16,3,81920]{2,0,1:T(8,128)(2,1)S(1)} async-done(((bf16[16,3,82048]{2,0,1:T(8,128)(2,1)}), bf16[16,3,81920]{2,0,1:T(8,128)(2,1)S(1)}, s32[]{:S(2)}) %slice-start) | async-done | bytes 7864344 | tf_op jit(solution)/shard_map/while/body/eval_jaxpr/slice | solution.py:24
  248.5 4.6 %copy.136 = bf16[6,8,128,640]{3,2,1,0:T(8,128)(2,1)} copy(bf16[6,8,128,640]{3,1,2,0:T(8,128)(2,1)S(1)} %bitcast.72) | data formatting | bytes 15728640 | tf_op jit(solution)/shard_map/while
  253.1 3.7 %fusion.78 = (bf16[16,3,128,128]{3,2,0,1:T(8,128)(2,1)S(1)}, bf16[16,3,128,128]{3,2,0,1:T(8,128)(2,1)S(1)}, bf16[16,3,128,128]{3,2,0,1:T(8,128)(2,1)S(1)}, bf16[...) fusion(bf16[16,3,128,640]{3,2,0,1:T(8,128)(2,1)} %bitcast.73), kind=kLoop, calls=%fused_computation.70.clone.1 | loop fusion | bytes 15728640 | tf_op jit(solution)/shard_map/while/body/eval_jaxpr/slice | solution.py:58
  262.4 35.3 %while.14 = (s32[]{:T(128)}, f32[16,1024]{1,0:T(8,128)S(1)}, s32[16,2]{0,1:T(2,128)S(1)}, f32[16,768]{1,0:T(8,128)S(1)}, s32[]{:T(128)}, /*index=5*/s32[]{:T(128)}) while((s32[]{:T(128)}, f32[16,1024]{1,0:T(8,128)S(1)}, s32[16,2]{0,1:T(2,128)S(1)}, f32[16,768]{1,0:T(8,128)S(1)}, s32[]{:T(128)}, /*index=5*/s32[]{:T(128)}) %tuple.55), condition=%wide.while_cond, body=%wide.while_body.sunk | while | flops 2 | bytes 12401 | solution.py:66
  263.1 1.5 dynamic-slice.7
  274.1 1.5 dynamic-slice.7
  294.0 1.5 dynamic-slice.7
  298.4 1.6 reshape_reshape.15
  300.0 6.9 %all-to-all-start.3 = ((f32[16,3,768]{2,1,0:T(4,128)}), f32[16,3,768]{2,1,0:T(4,128)S(1)}, u32[]{:S(2)}, u32[]{:S(2)}) async-start(f32[16,3,768]{2,1,0:T(4,128)} %reshape_reshape.15), calls=%async_computation.3 | async-start | bytes 393216 | tf_op jit(solution)/shard_map/all_to_all | solution.py:149
  306.9 7.6 %all-to-all-done.3 = f32[16,3,768]{2,1,0:T(4,128)S(1)} async-done(((f32[16,3,768]{2,1,0:T(4,128)}), f32[16,3,768]{2,1,0:T(4,128)S(1)}, u32[]{:S(2)}, u32[]{:S(2)}) %all-to-all-start.3) | async-done | bytes 147488 | tf_op jit(solution)/shard_map/all_to_all | solution.py:149
  (274 shorter events, 92.3 us)
Async XLA Ops:
  0.0 39.5 %copy-start = (bf16[2,12,3,400]{3,0,2,1:T(2,128)(2,1)S(1)}, bf16[2,12,3,400]{3,0,2,1:T(2,128)(2,1)}, u32[]{:S(2)}) copy-start(bf16[2,12,3,400]{3,0,2,1:T(2,128)(2,1)} %param.7) | copy-start | bytes 172804
  3.2 36.3 %all-to-all-start = ((s32[16,1,3]{2,1,0:T(1,128)}), s32[16,1,3]{2,1,0:T(1,128)S(1)}, u32[]{:S(2)}, u32[]{:S(2)}) async-start(s32[16,1,3]{2,1,0:T(1,128)} %bitcast.7), calls=%async_computation | async-start | bytes 16384 | tf_op jit(solution)/shard_map/all_to_all | solution.py:130
  39.6 13.2 %all-to-all-start.2 = ((s32[16,1,3]{2,1,0:T(1,128)}), s32[16,1,3]{2,1,0:T(1,128)S(1)}, u32[]{:S(2)}, u32[]{:S(2)}) async-start(s32[16,1,3]{2,1,0:T(1,128)} %bitcast.11), calls=%async_computation.2 | async-start | bytes 16384 | tf_op jit(solution)/shard_map/all_to_all | solution.py:131
  52.8 22.3 %all-to-all-start.1 = ((bf16[16,3,3,400]{3,1,2,0:T(4,128)(2,1)}), bf16[16,3,3,400]{3,1,2,0:T(4,128)(2,1)S(1)}, u32[]{:S(2)}, u32[]{:S(2)}) async-start(bf16[16,3,3,400]{3,1,2,0:T(4,128)(2,1)} %copy.70), calls=%async_computation.1 | async-start | bytes 393216 | tf_op jit(solution)/shard_map/all_to_all | solution.py:129
  97.0 3.2 %slice-start = ((bf16[16,3,82048]{2,0,1:T(8,128)(2,1)}), bf16[16,3,81920]{2,0,1:T(8,128)(2,1)S(1)}, s32[]{:S(2)}) async-start(bf16[16,3,82048]{2,0,1:T(8,128)(2,1)} %tile.12), calls=%async_computation.4 | async-start | bytes 15728640 | tf_op jit(solution)/shard_map/while/body/eval_jaxpr/slice | solution.py:24
  171.1 3.2 %slice-start = ((bf16[16,3,82048]{2,0,1:T(8,128)(2,1)}), bf16[16,3,81920]{2,0,1:T(8,128)(2,1)S(1)}, s32[]{:S(2)}) async-start(bf16[16,3,82048]{2,0,1:T(8,128)(2,1)} %tile.12), calls=%async_computation.4 | async-start | bytes 15728640 | tf_op jit(solution)/shard_map/while/body/eval_jaxpr/slice | solution.py:24
  245.3 3.2 %slice-start = ((bf16[16,3,82048]{2,0,1:T(8,128)(2,1)}), bf16[16,3,81920]{2,0,1:T(8,128)(2,1)S(1)}, s32[]{:S(2)}) async-start(bf16[16,3,82048]{2,0,1:T(8,128)(2,1)} %tile.12), calls=%async_computation.4 | async-start | bytes 15728640 | tf_op jit(solution)/shard_map/while/body/eval_jaxpr/slice | solution.py:24
  300.0 14.5 %all-to-all-start.3 = ((f32[16,3,768]{2,1,0:T(4,128)}), f32[16,3,768]{2,1,0:T(4,128)S(1)}, u32[]{:S(2)}, u32[]{:S(2)}) async-start(f32[16,3,768]{2,1,0:T(4,128)} %reshape_reshape.15), calls=%async_computation.3 | async-start | bytes 393216 | tf_op jit(solution)/shard_map/all_to_all | solution.py:149
where the time goes:
time: 318 us; the launch traced here: 316 us
  local copies, waits for them, and re-layouts  217 us (68%)
  blocking collectives  39.1 us (12%)
  starting transfers between devices  24.9 us (8%)
  matrix products  13.8 us (4%)
  waiting for transfers between devices  11.5 us (4%)
  other arithmetic  8.16 us (3%)
    gather x192, local copies, waits for them, and re-layouts  105 us
    another operation x6, local copies, waits for them, and re-layouts, toeplitz(): repeated = jnp.tile(padded, (1,) * len(leading) + (frame_size,))  57.4 us
    all_gather x1, blocking collectives, shards(): group_scale = lax.all_gather(local_scale, 'tp', axis=0, tiled=True)  22.2 us
    all_gather x1, blocking collectives, shards(): group_rows = lax.all_gather(continuous, 'tp', axis=0, tiled=True)  16.9 us
    dot_general x15, matrix products, correlate(): jnp.einsum('ncbp,ncip->ncbi', frames[:, :, step_index:step_index + blocks...  13.8 us
    while x9, local copies, waits for them, and re-layouts  13.8 us
    slice x3, local copies, waits for them, and re-layouts, correlate(): bands[..., step_index * frame_size:(step_index + 1) * frame_size]  11.2 us
    slice x6, local copies, waits for them, and re-layouts, toeplitz(): repeated[..., :frame_size * row_width]  9.7 us
  transfers between devices with their start and end apart: 4, of which 2 were waited for; matrix products, arithmetic and copies ran while one was open for 3% of the time, Pallas kernels for 0%

commit v1 on v0

--- a/solution.py
+++ b/solution.py
@@ -97,7 +97,21 @@
     slot_index = owners * capacity + position
     flat_shift = moveouts.reshape(entries)
     flat_templates = templates.reshape(entries, CH, TLEN)
-    group_rows = lax.all_gather(continuous, "tp", axis=0, tiled=True)
+    ways, here, turn = (lax.axis_size("tp"), lax.axis_index("tp"), continuous.shape[0])
+    shape = [n * ways if d == 0 else n for d, n in enumerate(continuous.shape)]
+    full = lax.dynamic_update_slice_in_dim(
+        jnp.zeros(shape, continuous.dtype), continuous, here * turn, axis=0
+    )
+    going_up = going_down = continuous
+    for far in range(1, ways // 2 + 1):
+        going_up = lax.ppermute(going_up, "tp", [(d, (d + 1) % ways) for d in range(ways)])
+        full = lax.dynamic_update_slice_in_dim(full, going_up, (here - far) % ways * turn, axis=0)
+        if 2 * far < ways:
+            going_down = lax.ppermute(going_down, "tp", [(d, (d - 1) % ways) for d in range(ways)])
+            full = lax.dynamic_update_slice_in_dim(
+                full, going_down, (here + far) % ways * turn, axis=0
+            )
+    group_rows = full
     local_scale = inverse_level(continuous)
     group_scale = lax.all_gather(local_scale, "tp", axis=0, tiled=True)
     slot_templates = (

time: 318 us -> 321 us (level)
  starting transfers between devices: 24.9 us -> 47 us
  blocking collectives: 39.1 us -> 21.7 us
  local copies, waits for them, and re-layouts: 217 us -> 204 us
  waiting for transfers between devices: 11.5 us -> 20.1 us
    ppermute x0 -> x15, starting transfers between devices: none -> 23.2 us  [the longest x7 16.5 us: shards(): lax.ppermute(going_down, 'tp', [(d, (d - 1) % ways) for d in range(ways)])]
    all_gather x1 -> x0, blocking collectives: 16.9 us -> none  [shards(): group_rows = lax.all_gather(continuous, 'tp', axis=0, tiled=True)]
    gather x192, local copies, waits for them, and re-layouts: 105 us -> 92.1 us
    ppermute x0 -> x15, waiting for transfers between devices: none -> 7.82 us  [the longest x8 6.09 us: shards(): lax.ppermute(going_up, 'tp', [(d, (d + 1) % ways) for d in range(ways)])]
  transfers between devices with their start and end apart: 4 -> 19, of which waited for: 2 -> 12; matrix products, arithmetic and copies ran while one was open for 3% -> 4% of each run, Pallas kernels for 0% -> 0%
where the time goes in v1:
time: 321 us; the launch traced here: 317 us
  local copies, waits for them, and re-layouts  204 us (64%)
  starting transfers between devices  47 us (15%)
  blocking collectives  21.7 us (7%)
  waiting for transfers between devices  20.1 us (6%)
  matrix products  13.8 us (4%)
  other arithmetic  8.3 us (3%)
    gather x192, local copies, waits for them, and re-layouts  92.1 us
    another operation x6, local copies, waits for them, and re-layouts, toeplitz(): repeated = jnp.tile(padded, (1,) * len(leading) + (frame_size,))  57.4 us
    all_gather x1, blocking collectives, shards(): group_scale = lax.all_gather(local_scale, 'tp', axis=0, tiled=True)  21.7 us
    ppermute x7, starting transfers between devices, shards(): lax.ppermute(going_down, 'tp', [(d, (d - 1) % ways) for d in range(ways)])  16.5 us
    while x9, local copies, waits for them, and re-layouts  13.8 us
    dot_general x15, matrix products, correlate(): jnp.einsum('ncbp,ncip->ncbi', frames[:, :, step_index:step_index + blocks...  13.8 us
    slice x3, local copies, waits for them, and re-layouts, correlate(): bands[..., step_index * frame_size:(step_index + 1) * frame_size]  11.2 us
    slice x6, local copies, waits for them, and re-layouts, toeplitz(): repeated[..., :frame_size * row_width]  9.7 us
  transfers between devices with their start and end apart: 19, of which 12 were waited for; matrix products, arithmetic and copies ran while one was open for 4% of the time, Pallas kernels for 0%

profile of v1, /device:TPU:1, one launch (start us, length us, event | category | flops | bytes accessed | tf_op | source)
XLA Modules:
  0.0 316.6 jit_solution(2005104480942237494)
XLA Ops:
  0.9 3.0 collective-permute-start
  7.3 6.5 %all-to-all-start = ((s32[16,1,3]{2,1,0:T(1,128)}), s32[16,1,3]{2,1,0:T(1,128)S(1)}, u32[]{:S(2)}, u32[]{:S(2)}) async-start(s32[16,1,3]{2,1,0:T(1,128)} %bitcast.7), calls=%async_computation | async-start | bytes 16384 | tf_op jit(solution)/shard_map/all_to_all | solution.py:144
  14.7 1.7 reduce-window.6
  17.5 21.7 %all_gather.3 = f32[32,3,1024]{2,1,0:T(4,128)S(1)} all-gather(f32[2,3,1024]{2,1,0:T(4,128)S(1)} %copy.84), channel_id=1, replica_groups=mesh['st'=16,'tp'=16] {'tp'}, dimensions={0}, use_global_device_ids=true | all-gather | bytes 417792 | tf_op jit(solution)/shard_map/all_gather | solution.py:116
  40.8 1.5 scatter_fusion
  43.1 6.9 %all-to-all-start.2 = ((s32[16,1,3]{2,1,0:T(1,128)}), s32[16,1,3]{2,1,0:T(1,128)S(1)}, u32[]{:S(2)}, u32[]{:S(2)}) async-start(s32[16,1,3]{2,1,0:T(1,128)} %bitcast.11), calls=%async_computation.2 | async-start | bytes 16384 | tf_op jit(solution)/shard_map/all_to_all | solution.py:145
  51.3 5.1 %all-to-all-done.2 = s32[16,1,3]{2,1,0:T(1,128)S(1)} async-done(((s32[16,1,3]{2,1,0:T(1,128)}), s32[16,1,3]{2,1,0:T(1,128)S(1)}, u32[]{:S(2)}, u32[]{:S(2)}) %all-to-all-start.2) | async-done | bytes 224 | tf_op jit(solution)/shard_map/all_to_all | solution.py:145
  56.5 3.5 %all-to-all-start.1 = ((bf16[16,3,3,400]{3,1,2,0:T(4,128)(2,1)}), bf16[16,3,3,400]{3,1,2,0:T(4,128)(2,1)S(1)}, u32[]{:S(2)}, u32[]{:S(2)}) async-start(bf16[16,3,3,400]{3,1,2,0:T(4,128)(2,1)} %copy.78), calls=%async_computation.1 | async-start | bytes 393216 | tf_op jit(solution)/shard_map/all_to_all | solution.py:143
  62.9 2.0 collective-permute-start.4
  64.9 1.8 collective-permute-start.5
  68.4 3.0 collective-permute-start.7
  72.3 3.6 %collective-permute-start.9 = (bf16[2,3,1424]{2,1,0:T(4,128)(2,1)S(1)}, bf16[2,3,1424]{2,1,0:T(4,128)(2,1)S(1)}, u32[]{:S(2)}, u32[]{:S(2)}) collective-permute-start(bf16[2,3,1424]{2,1,0:T(4,128)(2,1)S(1)} %collective-permute-done.7), channel_id=1, source_target_pairs={{0,15},{1,0},{2,1},{3,2},{4,3},{5,4},{6,5},{7,6},{8,7},{9,8},{10,9... | collective-permute-start | bytes 51272 | tf_op jit(solution)/shard_map/ppermute | solution.py:110
  76.7 3.6 %collective-permute-start.11 = (bf16[2,3,1424]{2,1,0:T(4,128)(2,1)S(1)}, bf16[2,3,1424]{2,1,0:T(4,128)(2,1)S(1)}, u32[]{:S(2)}, u32[]{:S(2)}) collective-permute-start(bf16[2,3,1424]{2,1,0:T(4,128)(2,1)S(1)} %collective-permute-done.9), channel_id=1, source_target_pairs={{0,15},{1,0},{2,1},{3,2},{4,3},{5,4},{6,5},{7,6},{8,7},{9,8},{10,9... | collective-permute-start | bytes 51272 | tf_op jit(solution)/shard_map/ppermute | solution.py:110
  81.2 3.6 %collective-permute-start.13 = (bf16[2,3,1424]{2,1,0:T(4,128)(2,1)S(1)}, bf16[2,3,1424]{2,1,0:T(4,128)(2,1)S(1)}, u32[]{:S(2)}, u32[]{:S(2)}) collective-permute-start(bf16[2,3,1424]{2,1,0:T(4,128)(2,1)S(1)} %collective-permute-done.11), channel_id=1, source_target_pairs={{0,15},{1,0},{2,1},{3,2},{4,3},{5,4},{6,5},{7,6},{8,7},{9,8},{10,9... | collective-permute-start | bytes 51272 | tf_op jit(solution)/shard_map/ppermute | solution.py:110
  85.8 3.9 %collective-permute-done.14 = bf16[2,3,1424]{2,1,0:T(4,128)(2,1)S(1)} collective-permute-done((bf16[2,3,1424]{2,1,0:T(4,128)(2,1)S(1)}, bf16[2,3,1424]{2,1,0:T(4,128)(2,1)S(1)}, u32[]{:S(2)}, u32[]{:S(2)}) %collective-permute-start.14) | collective-permute-done | bytes 17120 | tf_op jit(solution)/shard_map/ppermute | solution.py:107
  89.7 209.9 %while.13 = (s32[]{:T(128)}, f32[3,16,768]{2,1,0:T(8,128)}, s32[3,16]{1,0:T(4,128)S(1)}, bf16[32,3,1424]{2,1,0:T(4,128)(2,1)S(1)}, bf16[3,16,3,400]{3,1,0,2:T(8,...) while((s32[]{:T(128)}, f32[3,16,768]{2,1,0:T(8,128)}, ...), condition=%wide.region_10.11_spmd, body=%wide.region_7.10_spmd.sunk | while | flops 63301088 | bytes 91004616 | solution.py:77
  91.6 4.3 %tile.11 = bf16[16,3,128,641]{3,2,0,1:T(8,128)(2,1)} broadcast(bf16[16,3,641]{2,0,1:T(8,128)(2,1)S(1)} %concatenate.21), dimensions={0,1,3} | broadcast | bytes 7938144 | tf_op jit(solution)/shard_map/while/body/eval_jaxpr/tile | solution.py:23
  95.9 14.9 %tile.12 = bf16[16,3,82048]{2,0,1:T(8,128)(2,1)} reshape(bf16[16,3,128,641]{3,2,0,1:T(8,128)(2,1)} %tile.11) | data formatting | bytes 15753216 | tf_op jit(solution)/shard_map/while/body/eval_jaxpr/tile | solution.py:23
  110.8 3.2 %slice-done = bf16[16,3,81920]{2,0,1:T(8,128)(2,1)S(1)} async-done(((bf16[16,3,82048]{2,0,1:T(8,128)(2,1)}), bf16[16,3,81920]{2,0,1:T(8,128)(2,1)S(1)}, s32[]{:S(2)}) %slice-start) | async-done | bytes 7864344 | tf_op jit(solution)/shard_map/while/body/eval_jaxpr/slice | solution.py:24
  114.0 4.6 %copy.146 = bf16[6,8,128,640]{3,2,1,0:T(8,128)(2,1)} copy(bf16[6,8,128,640]{3,1,2,0:T(8,128)(2,1)S(1)} %bitcast.72) | data formatting | bytes 15728640 | tf_op jit(solution)/shard_map/while
  118.6 3.7 %fusion.79 = (bf16[16,3,128,128]{3,2,0,1:T(8,128)(2,1)S(1)}, bf16[16,3,128,128]{3,2,0,1:T(8,128)(2,1)S(1)}, bf16[16,3,128,128]{3,2,0,1:T(8,128)(2,1)S(1)}, bf16[...) fusion(bf16[16,3,128,640]{3,2,0,1:T(8,128)(2,1)} %bitcast.73), kind=kLoop, calls=%fused_computation.86.clone.1 | loop fusion | bytes 15728640 | tf_op jit(solution)/shard_map/while/body/eval_jaxpr/slice | solution.py:58
  127.9 31.1 %while.14 = (s32[]{:T(128)}, f32[16,1024]{1,0:T(8,128)S(1)}, s32[16,2]{0,1:T(2,128)S(1)}, f32[16,768]{1,0:T(8,128)S(1)}, s32[]{:T(128)}, /*index=5*/s32[]{:T(128)}) while((s32[]{:T(128)}, f32[16,1024]{1,0:T(8,128)S(1)}, s32[16,2]{0,1:T(2,128)S(1)}, f32[16,768]{1,0:T(8,128)S(1)}, s32[]{:T(128)}, /*index=5*/s32[]{:T(128)}) %tuple.56), condition=%wide.while_cond, body=%wide.while_body.sunk | while | flops 2 | bytes 12401 | solution.py:66
  128.6 1.3 dynamic-slice.7
  130.5 1.3 dynamic-slice.7
  132.4 1.3 dynamic-slice.7
  134.4 1.3 dynamic-slice.7
  136.3 1.3 dynamic-slice.7
  138.3 1.3 dynamic-slice.7
  140.2 1.3 dynamic-slice.7
  142.2 1.3 dynamic-slice.7
  146.0 1.3 dynamic-slice.7
  148.0 1.3 dynamic-slice.7
  149.9 1.3 dynamic-slice.7
  151.9 1.3 dynamic-slice.7
  153.8 1.3 dynamic-slice.7
  155.8 1.3 dynamic-slice.7
  157.7 1.3 dynamic-slice.7
  161.6 4.3 %tile.11 = bf16[16,3,128,641]{3,2,0,1:T(8,128)(2,1)} broadcast(bf16[16,3,641]{2,0,1:T(8,128)(2,1)S(1)} %concatenate.21), dimensions={0,1,3} | broadcast | bytes 7938144 | tf_op jit(solution)/shard_map/while/body/eval_jaxpr/tile | solution.py:23
  165.8 14.9 %tile.12 = bf16[16,3,82048]{2,0,1:T(8,128)(2,1)} reshape(bf16[16,3,128,641]{3,2,0,1:T(8,128)(2,1)} %tile.11) | data formatting | bytes 15753216 | tf_op jit(solution)/shard_map/while/body/eval_jaxpr/tile | solution.py:23
  180.7 3.2 %slice-done = bf16[16,3,81920]{2,0,1:T(8,128)(2,1)S(1)} async-done(((bf16[16,3,82048]{2,0,1:T(8,128)(2,1)}), bf16[16,3,81920]{2,0,1:T(8,128)(2,1)S(1)}, s32[]{:S(2)}) %slice-start) | async-done | bytes 7864344 | tf_op jit(solution)/shard_map/while/body/eval_jaxpr/slice | solution.py:24
  184.0 4.6 %copy.146 = bf16[6,8,128,640]{3,2,1,0:T(8,128)(2,1)} copy(bf16[6,8,128,640]{3,1,2,0:T(8,128)(2,1)S(1)} %bitcast.72) | data formatting | bytes 15728640 | tf_op jit(solution)/shard_map/while
  188.5 3.7 %fusion.79 = (bf16[16,3,128,128]{3,2,0,1:T(8,128)(2,1)S(1)}, bf16[16,3,128,128]{3,2,0,1:T(8,128)(2,1)S(1)}, bf16[16,3,128,128]{3,2,0,1:T(8,128)(2,1)S(1)}, bf16[...) fusion(bf16[16,3,128,640]{3,2,0,1:T(8,128)(2,1)} %bitcast.73), kind=kLoop, calls=%fused_computation.86.clone.1 | loop fusion | bytes 15728640 | tf_op jit(solution)/shard_map/while/body/eval_jaxpr/slice | solution.py:58
  197.9 31.1 %while.14 = (s32[]{:T(128)}, f32[16,1024]{1,0:T(8,128)S(1)}, s32[16,2]{0,1:T(2,128)S(1)}, f32[16,768]{1,0:T(8,128)S(1)}, s32[]{:T(128)}, /*index=5*/s32[]{:T(128)}) while((s32[]{:T(128)}, f32[16,1024]{1,0:T(8,128)S(1)}, s32[16,2]{0,1:T(2,128)S(1)}, f32[16,768]{1,0:T(8,128)S(1)}, s32[]{:T(128)}, /*index=5*/s32[]{:T(128)}) %tuple.56), condition=%wide.while_cond, body=%wide.while_body.sunk | while | flops 2 | bytes 12401 | solution.py:66
  198.5 1.3 dynamic-slice.7
  200.5 1.3 dynamic-slice.7
  202.4 1.3 dynamic-slice.7
  204.3 1.3 dynamic-slice.7
  206.3 1.3 dynamic-slice.7
  208.2 1.3 dynamic-slice.7
  210.2 1.3 dynamic-slice.7
  212.1 1.3 dynamic-slice.7
  214.1 1.3 dynamic-slice.7
  216.0 1.3 dynamic-slice.7
  217.9 1.3 dynamic-slice.7
  219.9 1.3 dynamic-slice.7
  231.5 4.3 %tile.11 = bf16[16,3,128,641]{3,2,0,1:T(8,128)(2,1)} broadcast(bf16[16,3,641]{2,0,1:T(8,128)(2,1)S(1)} %concatenate.21), dimensions={0,1,3} | broadcast | bytes 7938144 | tf_op jit(solution)/shard_map/while/body/eval_jaxpr/tile | solution.py:23
  235.8 14.9 %tile.12 = bf16[16,3,82048]{2,0,1:T(8,128)(2,1)} reshape(bf16[16,3,128,641]{3,2,0,1:T(8,128)(2,1)} %tile.11) | data formatting | bytes 15753216 | tf_op jit(solution)/shard_map/while/body/eval_jaxpr/tile | solution.py:23
  250.7 3.2 %slice-done = bf16[16,3,81920]{2,0,1:T(8,128)(2,1)S(1)} async-done(((bf16[16,3,82048]{2,0,1:T(8,128)(2,1)}), bf16[16,3,81920]{2,0,1:T(8,128)(2,1)S(1)}, s32[]{:S(2)}) %slice-start) | async-done | bytes 7864344 | tf_op jit(solution)/shard_map/while/body/eval_jaxpr/slice | solution.py:24
  253.9 4.6 %copy.146 = bf16[6,8,128,640]{3,2,1,0:T(8,128)(2,1)} copy(bf16[6,8,128,640]{3,1,2,0:T(8,128)(2,1)S(1)} %bitcast.72) | data formatting | bytes 15728640 | tf_op jit(solution)/shard_map/while
  258.5 3.7 %fusion.79 = (bf16[16,3,128,128]{3,2,0,1:T(8,128)(2,1)S(1)}, bf16[16,3,128,128]{3,2,0,1:T(8,128)(2,1)S(1)}, bf16[16,3,128,128]{3,2,0,1:T(8,128)(2,1)S(1)}, bf16[...) fusion(bf16[16,3,128,640]{3,2,0,1:T(8,128)(2,1)} %bitcast.73), kind=kLoop, calls=%fused_computation.86.clone.1 | loop fusion | bytes 15728640 | tf_op jit(solution)/shard_map/while/body/eval_jaxpr/slice | solution.py:58
  267.8 31.1 %while.14 = (s32[]{:T(128)}, f32[16,1024]{1,0:T(8,128)S(1)}, s32[16,2]{0,1:T(2,128)S(1)}, f32[16,768]{1,0:T(8,128)S(1)}, s32[]{:T(128)}, /*index=5*/s32[]{:T(128)}) while((s32[]{:T(128)}, f32[16,1024]{1,0:T(8,128)S(1)}, s32[16,2]{0,1:T(2,128)S(1)}, f32[16,768]{1,0:T(8,128)S(1)}, s32[]{:T(128)}, /*index=5*/s32[]{:T(128)}) %tuple.56), condition=%wide.while_cond, body=%wide.while_body.sunk | while | flops 2 | bytes 12401 | solution.py:66
  299.6 1.6 reshape_reshape.15
  301.2 6.9 %all-to-all-start.3 = ((f32[16,3,768]{2,1,0:T(4,128)}), f32[16,3,768]{2,1,0:T(4,128)S(1)}, u32[]{:S(2)}, u32[]{:S(2)}) async-start(f32[16,3,768]{2,1,0:T(4,128)} %reshape_reshape.15), calls=%async_computation.3 | async-start | bytes 393216 | tf_op jit(solution)/shard_map/all_to_all | solution.py:163
  308.1 7.2 %all-to-all-done.3 = f32[16,3,768]{2,1,0:T(4,128)S(1)} async-done(((f32[16,3,768]{2,1,0:T(4,128)}), f32[16,3,768]{2,1,0:T(4,128)S(1)}, u32[]{:S(2)}, u32[]{:S(2)}) %all-to-all-start.3) | async-done | bytes 147488 | tf_op jit(solution)/shard_map/all_to_all | solution.py:163
  (321 shorter events, 101.4 us)
Async XLA Ops:
  0.0 39.3 %copy-start.1 = (s32[2,12]{1,0:T(2,128)S(1)}, s32[2,12]{1,0:T(2,128)}, u32[]{:S(2)}) copy-start(s32[2,12]{1,0:T(2,128)} %param.9) | copy-start | bytes 292
  0.0 40.7 %copy-start = (bf16[2,12,3,400]{3,0,2,1:T(2,128)(2,1)S(1)}, bf16[2,12,3,400]{3,0,2,1:T(2,128)(2,1)}, u32[]{:S(2)}) copy-start(bf16[2,12,3,400]{3,0,2,1:T(2,128)(2,1)} %param.7) | copy-start | bytes 172804
  0.9 59.9 %collective-permute-start = (bf16[2,3,1424]{2,1,0:T(4,128)(2,1)S(1)}, bf16[2,3,1424]{2,1,0:T(4,128)(2,1)S(1)}, u32[]{:S(2)}, u32[]{:S(2)}) collective-permute-start(bf16[2,3,1424]{2,1,0:T(4,128)(2,1)S(1)} %get-tuple-element.105), channel_id=1, source_target_pairs={{0,1},{1,2},{2,3},{3,4},{4,5},{5,6},{6,7},{7,8},{8,9},{9,10},{10,1... | collective-permute-start | bytes 51272 | tf_op jit(solution)/shard_map/ppermute | solution.py:107
  3.9 57.7 %collective-permute-start.1 = (bf16[2,3,1424]{2,1,0:T(4,128)(2,1)S(1)}, bf16[2,3,1424]{2,1,0:T(4,128)(2,1)S(1)}, u32[]{:S(2)}, u32[]{:S(2)}) collective-permute-start(bf16[2,3,1424]{2,1,0:T(4,128)(2,1)S(1)} %get-tuple-element.105), channel_id=1, source_target_pairs={{0,15},{1,0},{2,1},{3,2},{4,3},{5,4},{6,5},{7,6},{8,7},{9,8},{10,9... | collective-permute-start | bytes 51272 | tf_op jit(solution)/shard_map/ppermute | solution.py:110
  7.3 35.8 %all-to-all-start = ((s32[16,1,3]{2,1,0:T(1,128)}), s32[16,1,3]{2,1,0:T(1,128)S(1)}, u32[]{:S(2)}, u32[]{:S(2)}) async-start(s32[16,1,3]{2,1,0:T(1,128)} %bitcast.7), calls=%async_computation | async-start | bytes 16384 | tf_op jit(solution)/shard_map/all_to_all | solution.py:144
  43.1 13.4 %all-to-all-start.2 = ((s32[16,1,3]{2,1,0:T(1,128)}), s32[16,1,3]{2,1,0:T(1,128)S(1)}, u32[]{:S(2)}, u32[]{:S(2)}) async-start(s32[16,1,3]{2,1,0:T(1,128)} %bitcast.11), calls=%async_computation.2 | async-start | bytes 16384 | tf_op jit(solution)/shard_map/all_to_all | solution.py:145
  56.5 28.4 %all-to-all-start.1 = ((bf16[16,3,3,400]{3,1,2,0:T(4,128)(2,1)}), bf16[16,3,3,400]{3,1,2,0:T(4,128)(2,1)S(1)}, u32[]{:S(2)}, u32[]{:S(2)}) async-start(bf16[16,3,3,400]{3,1,2,0:T(4,128)(2,1)} %copy.78), calls=%async_computation.1 | async-start | bytes 393216 | tf_op jit(solution)/shard_map/all_to_all | solution.py:143
  60.7 2.1 collective-permute-start.2
  61.6 3.3 %collective-permute-start.3 = (bf16[2,3,1424]{2,1,0:T(4,128)(2,1)S(1)}, bf16[2,3,1424]{2,1,0:T(4,128)(2,1)S(1)}, u32[]{:S(2)}, u32[]{:S(2)}) collective-permute-start(bf16[2,3,1424]{2,1,0:T(4,128)(2,1)S(1)} %collective-permute-done.1), channel_id=1, source_target_pairs={{0,15},{1,0},{2,1},{3,2},{4,3},{5,4},{6,5},{7,6},{8,7},{9,8},{10,9... | collective-permute-start | bytes 51272 | tf_op jit(solution)/shard_map/ppermute | solution.py:110
  62.9 4.5 %collective-permute-start.4 = (bf16[2,3,1424]{2,1,0:T(4,128)(2,1)S(1)}, bf16[2,3,1424]{2,1,0:T(4,128)(2,1)S(1)}, u32[]{:S(2)}, u32[]{:S(2)}) collective-permute-start(bf16[2,3,1424]{2,1,0:T(4,128)(2,1)S(1)} %collective-permute-done.2), channel_id=1, source_target_pairs={{0,1},{1,2},{2,3},{3,4},{4,5},{5,6},{6,7},{7,8},{8,9},{9,10},{10,1... | collective-permute-start | bytes 51272 | tf_op jit(solution)/shard_map/ppermute | solution.py:107
  64.9 3.5 %collective-permute-start.5 = (bf16[2,3,1424]{2,1,0:T(4,128)(2,1)S(1)}, bf16[2,3,1424]{2,1,0:T(4,128)(2,1)S(1)}, u32[]{:S(2)}, u32[]{:S(2)}) collective-permute-start(bf16[2,3,1424]{2,1,0:T(4,128)(2,1)S(1)} %collective-permute-done.3), channel_id=1, source_target_pairs={{0,15},{1,0},{2,1},{3,2},{4,3},{5,4},{6,5},{7,6},{8,7},{9,8},{10,9... | collective-permute-start | bytes 51272 | tf_op jit(solution)/shard_map/ppermute | solution.py:110
  67.3 4.5 %collective-permute-start.6 = (bf16[2,3,1424]{2,1,0:T(4,128)(2,1)S(1)}, bf16[2,3,1424]{2,1,0:T(4,128)(2,1)S(1)}, u32[]{:S(2)}, u32[]{:S(2)}) collective-permute-start(bf16[2,3,1424]{2,1,0:T(4,128)(2,1)S(1)} %collective-permute-done.4), channel_id=1, source_target_pairs={{0,1},{1,2},{2,3},{3,4},{4,5},{5,6},{6,7},{7,8},{8,9},{9,10},{10,1... | collective-permute-start | bytes 51272 | tf_op jit(solution)/shard_map/ppermute | solution.py:107
  68.4 3.9 %collective-permute-start.7 = (bf16[2,3,1424]{2,1,0:T(4,128)(2,1)S(1)}, bf16[2,3,1424]{2,1,0:T(4,128)(2,1)S(1)}, u32[]{:S(2)}, u32[]{:S(2)}) collective-permute-start(bf16[2,3,1424]{2,1,0:T(4,128)(2,1)S(1)} %collective-permute-done.5), channel_id=1, source_target_pairs={{0,15},{1,0},{2,1},{3,2},{4,3},{5,4},{6,5},{7,6},{8,7},{9,8},{10,9... | collective-permute-start | bytes 51272 | tf_op jit(solution)/shard_map/ppermute | solution.py:110
  71.8 4.5 %collective-permute-start.8 = (bf16[2,3,1424]{2,1,0:T(4,128)(2,1)S(1)}, bf16[2,3,1424]{2,1,0:T(4,128)(2,1)S(1)}, u32[]{:S(2)}, u32[]{:S(2)}) collective-permute-start(bf16[2,3,1424]{2,1,0:T(4,128)(2,1)S(1)} %collective-permute-done.6), channel_id=1, source_target_pairs={{0,1},{1,2},{2,3},{3,4},{4,5},{5,6},{6,7},{7,8},{8,9},{9,10},{10,1... | collective-permute-start | bytes 51272 | tf_op jit(solution)/shard_map/ppermute | solution.py:107
  72.3 4.5 %collective-permute-start.9 = (bf16[2,3,1424]{2,1,0:T(4,128)(2,1)S(1)}, bf16[2,3,1424]{2,1,0:T(4,128)(2,1)S(1)}, u32[]{:S(2)}, u32[]{:S(2)}) collective-permute-start(bf16[2,3,1424]{2,1,0:T(4,128)(2,1)S(1)} %collective-permute-done.7), channel_id=1, source_target_pairs={{0,15},{1,0},{2,1},{3,2},{4,3},{5,4},{6,5},{7,6},{8,7},{9,8},{10,9... | collective-permute-start | bytes 51272 | tf_op jit(solution)/shard_map/ppermute | solution.py:110
  76.3 4.5 %collective-permute-start.10 = (bf16[2,3,1424]{2,1,0:T(4,128)(2,1)S(1)}, bf16[2,3,1424]{2,1,0:T(4,128)(2,1)S(1)}, u32[]{:S(2)}, u32[]{:S(2)}) collective-permute-start(bf16[2,3,1424]{2,1,0:T(4,128)(2,1)S(1)} %collective-permute-done.8), channel_id=1, source_target_pairs={{0,1},{1,2},{2,3},{3,4},{4,5},{5,6},{6,7},{7,8},{8,9},{9,10},{10,1... | collective-permute-start | bytes 51272 | tf_op jit(solution)/shard_map/ppermute | solution.py:107
  76.7 4.5 %collective-permute-start.11 = (bf16[2,3,1424]{2,1,0:T(4,128)(2,1)S(1)}, bf16[2,3,1424]{2,1,0:T(4,128)(2,1)S(1)}, u32[]{:S(2)}, u32[]{:S(2)}) collective-permute-start(bf16[2,3,1424]{2,1,0:T(4,128)(2,1)S(1)} %collective-permute-done.9), channel_id=1, source_target_pairs={{0,15},{1,0},{2,1},{3,2},{4,3},{5,4},{6,5},{7,6},{8,7},{9,8},{10,9... | collective-permute-start | bytes 51272 | tf_op jit(solution)/shard_map/ppermute | solution.py:110
  80.7 5.0 %collective-permute-start.12 = (bf16[2,3,1424]{2,1,0:T(4,128)(2,1)S(1)}, bf16[2,3,1424]{2,1,0:T(4,128)(2,1)S(1)}, u32[]{:S(2)}, u32[]{:S(2)}) collective-permute-start(bf16[2,3,1424]{2,1,0:T(4,128)(2,1)S(1)} %collective-permute-done.10), channel_id=1, source_target_pairs={{0,1},{1,2},{2,3},{3,4},{4,5},{5,6},{6,7},{7,8},{8,9},{9,10},{10,1... | collective-permute-start | bytes 51272 | tf_op jit(solution)/shard_map/ppermute | solution.py:107
  81.2 4.6 %collective-permute-start.13 = (bf16[2,3,1424]{2,1,0:T(4,128)(2,1)S(1)}, bf16[2,3,1424]{2,1,0:T(4,128)(2,1)S(1)}, u32[]{:S(2)}, u32[]{:S(2)}) collective-permute-start(bf16[2,3,1424]{2,1,0:T(4,128)(2,1)S(1)} %collective-permute-done.11), channel_id=1, source_target_pairs={{0,15},{1,0},{2,1},{3,2},{4,3},{5,4},{6,5},{7,6},{8,7},{9,8},{10,9... | collective-permute-start | bytes 51272 | tf_op jit(solution)/shard_map/ppermute | solution.py:110
  85.7 3.9 %collective-permute-start.14 = (bf16[2,3,1424]{2,1,0:T(4,128)(2,1)S(1)}, bf16[2,3,1424]{2,1,0:T(4,128)(2,1)S(1)}, u32[]{:S(2)}, u32[]{:S(2)}) collective-permute-start(bf16[2,3,1424]{2,1,0:T(4,128)(2,1)S(1)} %collective-permute-done.12), channel_id=1, source_target_pairs={{0,1},{1,2},{2,3},{3,4},{4,5},{5,6},{6,7},{7,8},{8,9},{9,10},{10,1... | collective-permute-start | bytes 51272 | tf_op jit(solution)/shard_map/ppermute | solution.py:107
  110.8 3.2 %slice-start = ((bf16[16,3,82048]{2,0,1:T(8,128)(2,1)}), bf16[16,3,81920]{2,0,1:T(8,128)(2,1)S(1)}, s32[]{:S(2)}) async-start(bf16[16,3,82048]{2,0,1:T(8,128)(2,1)} %tile.12), calls=%async_computation.4 | async-start | bytes 15728640 | tf_op jit(solution)/shard_map/while/body/eval_jaxpr/slice | solution.py:24
  180.7 3.2 %slice-start = ((bf16[16,3,82048]{2,0,1:T(8,128)(2,1)}), bf16[16,3,81920]{2,0,1:T(8,128)(2,1)S(1)}, s32[]{:S(2)}) async-start(bf16[16,3,82048]{2,0,1:T(8,128)(2,1)} %tile.12), calls=%async_computation.4 | async-start | bytes 15728640 | tf_op jit(solution)/shard_map/while/body/eval_jaxpr/slice | solution.py:24
  250.7 3.2 %slice-start = ((bf16[16,3,82048]{2,0,1:T(8,128)(2,1)}), bf16[16,3,81920]{2,0,1:T(8,128)(2,1)S(1)}, s32[]{:S(2)}) async-start(bf16[16,3,82048]{2,0,1:T(8,128)(2,1)} %tile.12), calls=%async_computation.4 | async-start | bytes 15728640 | tf_op jit(solution)/shard_map/while/body/eval_jaxpr/slice | solution.py:24
  301.2 14.1 %all-to-all-start.3 = ((f32[16,3,768]{2,1,0:T(4,128)}), f32[16,3,768]{2,1,0:T(4,128)S(1)}, u32[]{:S(2)}, u32[]{:S(2)}) async-start(f32[16,3,768]{2,1,0:T(4,128)} %reshape_reshape.15), calls=%async_computation.3 | async-start | bytes 393216 | tf_op jit(solution)/shard_map/all_to_all | solution.py:163
